TPU v7x, 32 devices: a whole 2x2x4 slice. The times are simulated.
32 devices in a mesh: dp: 8 (over z, y), tensor: 4 (over x, core).
Axes of the slice: x: 2, y: 2, z: 4, core: 2. Of those that a mesh axis runs over, the one named last changes fastest.
Arguments:
- tokens: bfloat16 [12288, 768], P('dp', 'tensor'), may hold values from -6 to 6
- cotangent: bfloat16 [12288, 768], P('dp', 'tensor'), may hold values from -6 to 6
- seq_start: int32 [12288], P('dp'), may hold values from 0 to 384, as said below
- row_place: int32 [8, 1536], P('dp'), may hold values from 0 to 1535, each once within a row
- qkv_weight: bfloat16 [3, 768, 768], P(None, None, 'tensor'), may hold values from -0.21875 to 0.21875
- qv_bias: bfloat16 [2, 768], P(None, 'tensor'), may hold values from -1.5 to 1.5
- out_weight: bfloat16 [768, 768], P('tensor'), may hold values from -0.875 to 0.875
- out_bias: bfloat16 [768], replicated, may hold values from -1.5 to 1.5
- first_gain: bfloat16 [768], replicated, may hold values from 0.5 to 1.5
- first_shift: bfloat16 [768], replicated, may hold values from -1.5 to 1.5
- up_weight: bfloat16 [2, 768, 3072], P(None, None, 'tensor'), may hold values from -0.21875 to 0.21875
- up_bias: bfloat16 [2, 3072], P(None, 'tensor'), may hold values from -1.5 to 1.5
- down_weight: bfloat16 [3072, 768], P('tensor'), may hold values from -0.15625 to 0.15625
- down_bias: bfloat16 [768], replicated, may hold values from -1.5 to 1.5
- second_gain: bfloat16 [768], replicated, may hold values from 0.5 to 1.5
- second_shift: bfloat16 [768], replicated, may hold values from -1.5 to 1.5
Outputs:
- layer_out: bfloat16 [12288, 768], P('dp', 'tensor')
- input_grad: bfloat16 [12288, 768], P('dp', 'tensor')
- qkv_grad: float32 [3, 768, 768], P(None, 'dp', 'tensor')
- qv_bias_grad: float32 [2, 768], P(None, 'tensor')
- out_grad: float32 [768, 768], P('tensor', 'dp')
- out_bias_grad: float32 [768], P('dp')
- first_gain_grad: float32 [768], P('dp')
- first_shift_grad: float32 [768], P('dp')
- up_grad: float32 [2, 768, 3072], P(None, 'dp', 'tensor')
- up_bias_grad: float32 [2, 3072], P(None, 'tensor')
- down_grad: float32 [3072, 768], P('tensor', 'dp')
- down_bias_grad: float32 [768], P('dp')
- second_gain_grad: float32 [768], P('dp')
- second_shift_grad: float32 [768], P('dp')
Inputs may be any that keep to these rules, and one draw needn't show every extreme that they name: seq_start of a token is the offset, within its aligned block of 512 packed rows, of the first token of its sequence; sequences are 128, 256 or 512 tokens long, begin at multiples of 128 and never cross a block. Each row of row_place is a permutation of 0 to 1535.
All inputs are finite; a program needn't handle non-finite values.
Results may differ from a plain program's by a relative error of at most 0.02.
The roundings to bfloat16 on the way count: a program that leaves them out, or rounds other values in their place, can miss the bound.
Values may be sent and summed in bfloat16 or wider, within the bound.
A program may use at most 128 MiB of HBM per device.

v0:
```python
import jax
import jax.numpy as jnp
from jax import lax
from jax.sharding import PartitionSpec as P

HEADS = 12
HEAD_DIM = 64
BLOCK = 512


def layer_norm(values, scale_row, shift_row):
    center = values - jnp.mean(values, axis=-1, keepdims=True)
    spread = jnp.mean(center * center, axis=-1, keepdims=True)
    return center * lax.rsqrt(spread + 1e-05) * scale_row + shift_row


def gated_unit(gate_part, value_part):
    return jax.nn.gelu(gate_part, approximate=False) * value_part


def alibi_terms(part_index, local_heads, block_rows):
    heads_idx = (part_index * local_heads + jnp.arange(local_heads)).astype(jnp.float32)
    slopes = 2.0 ** (-8.0 * (heads_idx + 1.0) / HEADS)
    position = jnp.arange(block_rows).astype(jnp.float32)
    distance = jnp.abs(position[:, None] - position[None, :])
    return -slopes[:, None, None] * distance[None]


def block_scores(queries, key_rows, alibi_bias, same_seq, score_scale):
    raw_scores = jnp.einsum(
        "bqhe,bkhe->bhqk", queries, key_rows, preferred_element_type=jnp.float32
    )
    scored = raw_scores * score_scale + alibi_bias[None]
    return jnp.where(same_seq[:, None], scored, -1e30)


def softmax_rows(scored):
    row_max = jnp.max(scored, axis=-1, keepdims=True)
    exponent = jnp.exp(scored - row_max)
    denominator = jnp.sum(exponent, axis=-1, keepdims=True)
    return (exponent / denominator, row_max + jnp.log(denominator))


def on_device(
    tokens,
    cotangent,
    seq_start,
    row_place,
    qkv_weight,
    qv_bias,
    out_weight,
    out_bias,
    first_gain,
    first_shift,
    up_weight,
    up_bias,
    down_weight,
    down_bias,
    second_gain,
    second_shift,
):
    arr_tokens, arr_cot = (
        lax.all_to_all(tokens, "dp", split_axis=0, concat_axis=0, tiled=True),
        lax.all_to_all(cotangent, "dp", split_axis=0, concat_axis=0, tiled=True),
    )
    wide_tokens, wide_cot = (
        lax.all_gather(arr_tokens, "tensor", axis=1, tiled=True),
        lax.all_gather(arr_cot, "tensor", axis=1, tiled=True),
    )
    slot_index = row_place[0]
    packed_in = jnp.zeros_like(wide_tokens).at[slot_index].set(wide_tokens)
    packed_cot = jnp.zeros_like(wide_cot).at[slot_index].set(wide_cot)
    row_count = packed_in.shape[0]
    columns = packed_in.shape[1]
    local_heads = qkv_weight.shape[2] // HEAD_DIM
    block_rows = BLOCK
    blocks = row_count // block_rows
    part_index = lax.axis_index("tensor")
    col_count = columns // lax.axis_size("tensor")
    score_scale = HEAD_DIM ** (-0.5)
    alibi_bias = alibi_terms(part_index, local_heads, block_rows)
    block_starts = seq_start.reshape(blocks, block_rows)
    same_seq = block_starts[:, :, None] == block_starts[:, None, :]
    bias_rows = jnp.stack([qv_bias[0], jnp.zeros_like(qv_bias[0]), qv_bias[1]]).astype(jnp.float32)
    projected = jnp.einsum("td,kde->kte", packed_in, qkv_weight, preferred_element_type=jnp.float32)
    qkv_rows = (projected + bias_rows[:, None, :]).astype(jnp.bfloat16)
    split_heads = qkv_rows.reshape(3, blocks, block_rows, local_heads, HEAD_DIM)
    queries = split_heads[0]
    key_rows = split_heads[1]
    value_rows = split_heads[2]
    attn_probs, log_total = softmax_rows(
        block_scores(queries, key_rows, alibi_bias, same_seq, score_scale)
    )
    context = jnp.einsum(
        "bhqk,bkhe->bqhe",
        attn_probs.astype(jnp.bfloat16),
        value_rows,
        preferred_element_type=jnp.float32,
    )
    context = context.reshape(row_count, local_heads * HEAD_DIM).astype(jnp.bfloat16)
    attn_part = jnp.dot(context, out_weight, preferred_element_type=jnp.float32)
    attended = lax.psum(attn_part, "tensor")
    hidden = packed_in.astype(jnp.float32) + (attended + out_bias.astype(jnp.float32))
    normed, first_pull = jax.vjp(
        layer_norm, hidden, first_gain.astype(jnp.float32), first_shift.astype(jnp.float32)
    )
    normed_low = normed.astype(jnp.bfloat16)
    lifted = jnp.einsum("td,kdf->ktf", normed_low, up_weight, preferred_element_type=jnp.float32)
    lifted = lifted + up_bias.astype(jnp.float32)[:, None, :]
    gated_val, gate_pull = jax.vjp(gated_unit, lifted[0], lifted[1])
    gated_low = gated_val.astype(jnp.bfloat16)
    ffn_part = jnp.dot(gated_low, down_weight, preferred_element_type=jnp.float32)
    ffn_out = lax.psum(ffn_part.astype(jnp.bfloat16), "tensor").astype(jnp.float32)
    mixed_rows = normed + (ffn_out + down_bias.astype(jnp.float32))
    result, second_pull = jax.vjp(
        layer_norm, mixed_rows, second_gain.astype(jnp.float32), second_shift.astype(jnp.float32)
    )
    grad_scale = (row_count * lax.axis_size("dp")) ** (-0.5)
    d_mixed, d_second_gain, d_second_shift = second_pull(packed_cot.astype(jnp.float32))
    d_mixed_low = d_mixed.astype(jnp.bfloat16)
    g_down = jnp.einsum("tf,td->fd", gated_low, d_mixed_low, preferred_element_type=jnp.float32)
    g_down_bias = jnp.sum(d_mixed, axis=0)
    d_gated = jnp.einsum("td,fd->tf", d_mixed_low, down_weight, preferred_element_type=jnp.float32)
    d_gate, d_value = gate_pull(d_gated)
    d_lifted = jnp.stack([d_gate, d_value]).astype(jnp.bfloat16)
    g_up = jnp.einsum("td,ktf->kdf", normed_low, d_lifted, preferred_element_type=jnp.float32)
    g_up_bias = jnp.sum(d_lifted, axis=1, dtype=jnp.float32)
    d_normed_part = jnp.einsum(
        "ktf,kdf->td", d_lifted, up_weight, preferred_element_type=jnp.float32
    )
    d_normed = d_mixed + lax.psum(d_normed_part.astype(jnp.bfloat16), "tensor").astype(jnp.float32)
    d_hidden, d_first_gain, d_first_shift = first_pull(d_normed)
    d_hidden_low = d_hidden.astype(jnp.bfloat16)
    g_out = jnp.einsum("te,td->ed", context, d_hidden_low, preferred_element_type=jnp.float32)
    g_out_bias = jnp.sum(d_hidden, axis=0)
    d_context = jnp.einsum(
        "td,ed->te", d_hidden_low, out_weight, preferred_element_type=jnp.float32
    )
    d_context = d_context.astype(jnp.bfloat16).reshape(blocks, block_rows, local_heads, HEAD_DIM)
    probs_back = jnp.exp(
        block_scores(queries, key_rows, alibi_bias, same_seq, score_scale) - log_total
    )
    d_probs = jnp.einsum(
        "bqhe,bkhe->bhqk", d_context, value_rows, preferred_element_type=jnp.float32
    )
    g_values = jnp.einsum(
        "bhqk,bqhe->bkhe",
        probs_back.astype(jnp.bfloat16),
        d_context,
        preferred_element_type=jnp.float32,
    )
    center_term = jnp.sum(probs_back * d_probs, axis=-1, keepdims=True)
    d_scores = (probs_back * (d_probs - center_term)).astype(jnp.bfloat16)
    g_queries = (
        jnp.einsum("bhqk,bkhe->bqhe", d_scores, key_rows, preferred_element_type=jnp.float32)
        * score_scale
    )
    g_keys = (
        jnp.einsum("bhqk,bqhe->bkhe", d_scores, queries, preferred_element_type=jnp.float32)
        * score_scale
    )
    d_qkv = jnp.stack([g_queries, g_keys, g_values]).reshape(3, row_count, local_heads * HEAD_DIM)
    d_qkv = d_qkv.astype(jnp.bfloat16)
    g_qkv = jnp.einsum("td,kte->kde", packed_in, d_qkv, preferred_element_type=jnp.float32)
    g_qv_bias = jnp.sum(jnp.stack([d_qkv[0], d_qkv[2]]), axis=1, dtype=jnp.float32)
    d_input_part = jnp.einsum("kte,kde->td", d_qkv, qkv_weight, preferred_element_type=jnp.float32)
    hidden_cols = lax.dynamic_slice_in_dim(d_hidden, part_index * col_count, col_count, 1)
    grad_cols = hidden_cols + lax.psum_scatter(
        d_input_part.astype(jnp.bfloat16), "tensor", scatter_dimension=1, tiled=True
    ).astype(jnp.float32)
    summed = (
        lax.psum_scatter(g_qkv * grad_scale, "dp", scatter_dimension=1, tiled=True),
        lax.psum_scatter(g_out * grad_scale, "dp", scatter_dimension=1, tiled=True),
        lax.psum_scatter(g_out_bias * grad_scale, "dp", scatter_dimension=0, tiled=True),
        lax.psum_scatter(d_first_gain * grad_scale, "dp", scatter_dimension=0, tiled=True),
        lax.psum_scatter(d_first_shift * grad_scale, "dp", scatter_dimension=0, tiled=True),
        lax.psum_scatter(g_up * grad_scale, "dp", scatter_dimension=1, tiled=True),
        lax.psum_scatter(g_down * grad_scale, "dp", scatter_dimension=1, tiled=True),
        lax.psum_scatter(g_down_bias * grad_scale, "dp", scatter_dimension=0, tiled=True),
        lax.psum_scatter(d_second_gain * grad_scale, "dp", scatter_dimension=0, tiled=True),
        lax.psum_scatter(d_second_shift * grad_scale, "dp", scatter_dimension=0, tiled=True),
    )
    qkv_grad, out_grad, out_bias_grad, first_gain_grad, first_shift_grad = (
        summed[0],
        summed[1],
        summed[2],
        summed[3],
        summed[4],
    )
    up_grad, down_grad, down_bias_grad, second_gain_grad, second_shift_grad = (
        summed[5],
        summed[6],
        summed[7],
        summed[8],
        summed[9],
    )
    qv_bias_grad, up_bias_grad = lax.psum((g_qv_bias * grad_scale, g_up_bias * grad_scale), "dp")
    layer_cols = lax.dynamic_slice_in_dim(result, part_index * col_count, col_count, 1)
    layer_back = layer_cols[slot_index].astype(jnp.bfloat16)
    grad_back = grad_cols[slot_index].astype(jnp.bfloat16)
    layer_out, input_grad = (
        lax.all_to_all(layer_back, "dp", split_axis=0, concat_axis=0, tiled=True),
        lax.all_to_all(grad_back, "dp", split_axis=0, concat_axis=0, tiled=True),
    )
    return (
        layer_out,
        input_grad,
        qkv_grad,
        qv_bias_grad,
        out_grad,
        out_bias_grad,
        first_gain_grad,
        first_shift_grad,
        up_grad,
        up_bias_grad,
        down_grad,
        down_bias_grad,
        second_gain_grad,
        second_shift_grad,
    )


def solution(mesh):
    return jax.shard_map(
        on_device,
        mesh=mesh,
        in_specs=(
            P("dp", "tensor"),
            P("dp", "tensor"),
            P("dp"),
            P("dp", None),
            P(None, None, "tensor"),
            P(None, "tensor"),
            P("tensor", None),
            P(),
            P(),
            P(),
            P(None, None, "tensor"),
            P(None, "tensor"),
            P("tensor", None),
            P(),
            P(),
            P(),
        ),
        out_specs=(
            P("dp", "tensor"),
            P("dp", "tensor"),
            P(None, "dp", "tensor"),
            P(None, "tensor"),
            P("tensor", "dp"),
            P("dp"),
            P("dp"),
            P("dp"),
            P(None, "dp", "tensor"),
            P(None, "tensor"),
            P("tensor", "dp"),
            P("dp"),
            P("dp"),
            P("dp"),
        ),
        check_vma=False,
    )
```

profile of v0, /device:TPU:0, one launch (start us, length us, event | category | flops | bytes accessed | tf_op | source)
XLA Modules:
  0.0 849.5 jit_solution(2268085062084630268)
XLA Ops:
  9.3 27.3 %all_to_all.42 = bf16[8,192,192]{1,2,0:T(8,128)(2,1)S(1)} all-to-all(bf16[8,192,192]{1,2,0:T(8,128)(2,1)S(1)} %copy.124), channel_id=1, replica_groups=mesh['dp'=8,'tensor'=4] {'dp'}, dimensions={0} | all-to-all | bytes 1179648 | tf_op jit(solution)/shard_map/all_to_all | solution.py:63
  42.5 19.2 %all-gather.3.cloned.1.call-done = bf16[1536,768]{0,1:T(8,128)(2,1)} async-done(((bf16[1536,192]{0,1:T(8,128)(2,1)}), bf16[1536,768]{0,1:T(8,128)(2,1)}) %all-gather.3.cloned.1.call-update) | async-done | bytes 2359312 | tf_op jit(solution)/shard_map/all_gather | solution.py:67
  61.7 4.3 copy.126
  66.0 10.1 %scatter_custom_fusion = bf16[1536,768]{1,0:T(8,128)(2,1)} fusion(s32[1536]{0:T(1024)S(1)} %fusion.70, bf16[1536,768]{1,0:T(8,128)(2,1)} %copy.126, bf16[]{:T(256)} %constant.46.clone.1), kind=kCustom, calls=%fused_computation.108 | custom fusion | bytes 2359808 | tf_op jit(solution)/shard_map/scatter | solution.py:71
  76.1 3.2 fusion.86
  84.3 5.3 fusion.85
  95.9 2.9 fusion.87
  103.5 5.5 all-to-all-start.2
  109.2 20.5 %all-to-all-done.2 = bf16[8,192,192]{1,2,0:T(8,128)(2,1)} async-done(((bf16[8,192,192]{1,2,0:T(8,128)(2,1)}), bf16[8,192,192]{1,2,0:T(8,128)(2,1)}, u32[]{:S(2)}, u32[]{:S(2)}) %all-to-all-start.2) | async-done | bytes 589856 | tf_op jit(solution)/shard_map/all_to_all | solution.py:64
  134.9 58.2 %all-reduce.13.cloned.1.call-done = f32[1536,768]{1,0:T(8,128)} async-done(((f32[1536,768]{1,0:T(8,128)}), f32[1536,768]{1,0:T(8,128)}) %all-reduce.13.cloned.1.call-update) | async-done | bytes 4718608 | tf_op jit(solution)/shard_map/psum | solution.py:102
  193.1 3.8 fusion.82
  197.6 4.3 add_bitcast_fusion
  201.9 11.5 %multiply_convert_fusion.2 = (bf16[1536,768]{1,0:T(8,128)(2,1)S(1)}, f32[1536,768]{1,0:T(8,128)}) fusion(f32[2,1536,768]{2,1,0:T(8,128)S(1)} %add_bitcast_fusion), kind=kLoop, calls=%fused_computation.51 | loop fusion | flops 77856768 | bytes 16515072 | tf_op jit(solution)/shard_map/convert_element_type | solution.py:111
  214.9 3.5 convolution_convert_fusion
  219.5 4.3 copy.135
  223.7 9.8 %scatter_custom_fusion.1 = bf16[1536,768]{1,0:T(8,128)(2,1)} fusion(s32[1536]{0:T(1024)} %copy-done.29, bf16[1536,768]{1,0:T(8,128)(2,1)} %copy.135, bf16[]{:T(256)} %constant.46.clone.1), kind=kCustom, calls=%fused_computation.106 | custom fusion | bytes 2359808 | tf_op jit(solution)/shard_map/scatter | solution.py:72
  233.6 43.8 %all-reduce.15.cloned.1.call-done = bf16[1536,768]{1,0:T(8,128)(2,1)} async-done(((bf16[1536,768]{1,0:T(8,128)(2,1)}), bf16[1536,768]{1,0:T(8,128)(2,1)}) %all-reduce.15.cloned.1.call-update) | async-done | bytes 2359312 | tf_op jit(solution)/shard_map/psum | solution.py:113
  277.4 4.2 fusion.80
  281.7 2.7 fusion.4
  284.4 4.7 fusion.79
  289.2 7.1 fusion.36
  297.7 7.0 bitcast_convert_fusion.1
  305.8 54.8 %all-reduce.17.cloned.1.call-done = bf16[1536,768]{1,0:T(8,128)(2,1)} async-done(((bf16[1536,768]{1,0:T(8,128)(2,1)}), bf16[1536,768]{1,0:T(8,128)(2,1)}) %all-reduce.17.cloned.1.call-update) | async-done | bytes 2359312 | tf_op jit(solution)/shard_map/psum | solution.py:131
  360.6 6.5 multiply_reduce_fusion.1
  367.1 5.0 fusion.78
  376.9 5.3 fusion.48
  382.2 7.2 multiply_reduce_fusion
  389.4 11.2 %multiply_convert_fusion = bf16[3,3,512,512]{2,3,1,0:T(8,128)(2,1)} fusion(f32[3,3,512,512]{2,3,1,0:T(8,128)} %get-tuple-element.127, f32[3,3,512,512]{2,3,1,0:T(8,128)} %copy-done.2, f32[3,3,512]{2,1,0:T(4,128)S(1)} %get-tuple-element.126, f32[3,3,512]{2,1,0:T(4,128)S(1)} %copy-done.23), kind=kLoop, calls=%fused_computation.5 | loop fusion | flops 9437184 | bytes 23629824 | tf_op jit(solution)/shard_map/convert_element_type | solution.py:153
  400.6 4.0 fusion.51
  407.9 2.7 copy.140
  417.0 4.6 fusion.31
  421.7 3.1 convolution_multiply_fusion.3
  426.1 4.5 multiply_bitcast_fusion.1
  430.6 4.2 copy.162
  434.9 4.8 reshape.283
  439.8 9.6 %multiply_bitcast_fusion = f32[2,768,768]{1,2,0:T(8,128)} fusion(bf16[1,1536,768]{2,1,0:T(8,128)(2,1)} %get-tuple-element.114, bf16[1,1536,768]{2,1,0:T(8,128)(2,1)S(1)} %copy-done.19, f32[1536,768]{1,0:T(8,128)} %copy-done.3, f32[768]{0:T(1024)S(1)} %copy-done.34, f32[768]{0:T(1024)S(1)} %copy-done.28, f32[1536]{0:T(1024)S(1)} %fusion.68, ...), kind=kOutput, calls=%fused_computation.43 | convolution fusion | flops 3633315840 | bytes 14174208 | tf_op jit(solution)/shard_map/td,ktf->kdf/dot_general | solution.py:126
  449.4 8.3 copy.150
  459.3 6.0 convolution_multiply_fusion
  467.7 5.4 gather_fusion
  473.0 5.3 all-to-all-start.1
  479.6 3.1 convert_reduce_fusion
  482.7 17.3 %all-to-all-done.1 = bf16[8,192,192]{2,1,0:T(8,128)(2,1)S(1)} async-done(((bf16[8,192,192]{2,1,0:T(8,128)(2,1)}), bf16[8,192,192]{2,1,0:T(8,128)(2,1)S(1)}, u32[]{:S(2)}, u32[]{:S(2)}) %all-to-all-start.1) | async-done | bytes 589856 | tf_op jit(solution)/shard_map/all_to_all | solution.py:202
  504.7 5.4 gather_fusion.1
  510.0 3.7 all-to-all-start.3
  515.3 44.6 %all-reduce.7 = (f32[2,192]{1,0:T(2,128)}, f32[768]{0:T(1024)S(1)}, f32[768]{0:T(1024)S(1)}, f32[768]{0:T(1024)S(1)}, f32[2,768]{1,0:T(2,128)}, /*index=5*/f32[7...) all-reduce(f32[2,192]{1,0:T(2,128)S(1)} %broadcast_multiply_fusion.10, ...), channel_id=1, replica_groups=mesh['dp'=8,'tensor'=4] {'dp'}, use_global_device_ids=true, to_apply=%region_19.20 | all-reduce | flops 6528 | bytes 52224 | tf_op jit(solution)/shard_map/psum | solution.py:197
  565.0 32.5 %reduce-scatter.15.cloned.1.call-done = f32[96,576]{1,0:T(8,128)} async-done(((f32[768,576]{1,0:T(8,128)}), f32[96,576]{1,0:T(8,128)}) %reduce-scatter.15.cloned.1.call-update) | async-done | bytes 221200
  599.4 170.4 %all-reduce.19.cloned.1.call-done = f32[2,768,768]{2,0,1:T(2,128)} async-done(((f32[2,768,768]{2,0,1:T(2,128)}), f32[2,768,768]{2,0,1:T(2,128)}) %all-reduce.19.cloned.1.call-update) | async-done | bytes 4718608
  772.8 69.6 %reduce-scatter.11.cloned.1.call-done = f32[768,96]{0,1:T(8,128)} async-done(((f32[768,768]{0,1:T(8,128)}), f32[768,96]{0,1:T(8,128)}) %reduce-scatter.11.cloned.1.call-update) | async-done | bytes 294928 | tf_op jit(solution)/shard_map/reduce_scatter | solution.py:178
  (224 shorter events, 71.1 us)
Async XLA Ops:
  7.2 190.4 %copy-start = (bf16[2,768,768]{2,1,0:T(8,128)(2,1)S(1)}, bf16[2,768,768]{2,1,0:T(8,128)(2,1)}, u32[]{:S(2)}) copy-start(bf16[2,768,768]{2,1,0:T(8,128)(2,1)} %param.26) | copy-start | bytes 7077892
  7.2 31.4 %copy-start.39 = (s32[1536]{0:T(1024)S(1)}, s32[1536]{0:T(1024)}, u32[]{:S(2)}) copy-start(s32[1536]{0:T(1024)} %param.18) | copy-start | bytes 18436
  7.2 31.5 %copy-start.40 = (s32[1,1536]{1,0:T(1,128)S(1)}, s32[1,1536]{1,0:T(1,128)}, u32[]{:S(2)}) copy-start(s32[1,1536]{1,0:T(1,128)} %param.19) | copy-start | bytes 18436
  7.2 31.5 %copy-start.43 = (bf16[2,192]{1,0:T(2,128)(2,1)S(1)}, bf16[2,192]{1,0:T(2,128)(2,1)}, u32[]{:S(2)}) copy-start(bf16[2,192]{1,0:T(2,128)(2,1)} %param.21) | copy-start | bytes 2308
  7.2 54.5 %all-gather.3.cloned.1.call-start = ((), (), s32[]{:S(2)}) async-start(), calls=%async_computation.8 | async-start | bytes 2949120 | tf_op jit(solution)/shard_map/all_gather | solution.py:67
  38.5 154.5 %all-reduce.13.cloned.1.call-start = ((), (), s32[]{:S(2)}) async-start(), calls=%async_computation.9 | async-start | bytes 9437184 | tf_op jit(solution)/shard_map/psum | solution.py:102
  38.8 27.3 %copy-start.29 = (s32[1536]{0:T(1024)}, s32[1536]{0:T(1024)S(1)}, u32[]{:S(2)}) copy-start(s32[1536]{0:T(1024)S(1)} %fusion.70) | copy-start | bytes 18436
  40.4 35.7 %copy-start.51 = (bf16[3,768,192]{1,2,0:T(8,128)(2,1)S(1)}, bf16[3,768,192]{1,2,0:T(8,128)(2,1)}, u32[]{:S(2)}) copy-start(bf16[3,768,192]{1,2,0:T(8,128)(2,1)} %param.20) | copy-start | bytes 2654212
  84.3 5.3 copy-start.11
  98.9 10.2 %copy-start.45 = (bf16[768]{0:T(1024)(128)(2,1)S(1)}, bf16[768]{0:T(1024)(128)(2,1)}, u32[]{:S(2)}) copy-start(bf16[768]{0:T(1024)(128)(2,1)} %param.24) | copy-start | bytes 4612
  98.9 10.2 %copy-start.46 = (bf16[768]{0:T(1024)(128)(2,1)S(1)}, bf16[768]{0:T(1024)(128)(2,1)}, u32[]{:S(2)}) copy-start(bf16[768]{0:T(1024)(128)(2,1)} %param.25) | copy-start | bytes 4612
  98.9 10.3 %copy-start.47 = (bf16[768]{0:T(1024)(128)(2,1)S(1)}, bf16[768]{0:T(1024)(128)(2,1)}, u32[]{:S(2)}) copy-start(bf16[768]{0:T(1024)(128)(2,1)} %param.23) | copy-start | bytes 4612
  98.9 10.3 %copy-start.44 = (bf16[2,768]{1,0:T(2,128)(2,1)S(1)}, bf16[2,768]{1,0:T(2,128)(2,1)}, u32[]{:S(2)}) copy-start(bf16[2,768]{1,0:T(2,128)(2,1)} %param.27) | copy-start | bytes 9220
  103.5 26.2 %all-to-all-start.2 = ((bf16[8,192,192]{1,2,0:T(8,128)(2,1)}), bf16[8,192,192]{1,2,0:T(8,128)(2,1)}, u32[]{:S(2)}, u32[]{:S(2)}) async-start(bf16[8,192,192]{1,2,0:T(8,128)(2,1)} %copy.133), calls=%async_computation.2 | async-start | bytes 1572864 | tf_op jit(solution)/shard_map/all_to_all | solution.py:64
  109.1 110.4 %all-gather.5.cloned.1.call-start = ((), (), s32[]{:S(2)}) async-start(), calls=%async_computation.11 | async-start | bytes 2949120 | tf_op jit(solution)/shard_map/all_gather | solution.py:68
  109.1 258.0 %copy-start.27 = (f32[768]{0:T(1024)}, f32[768]{0:T(1024)S(1)}, u32[]{:S(2)}) copy-start(f32[768]{0:T(1024)S(1)} %convert_element_type.142) | copy-start | bytes 9220
  109.2 168.2 %copy-start.33 = (f32[768]{0:T(1024)}, f32[768]{0:T(1024)S(1)}, u32[]{:S(2)}) copy-start(f32[768]{0:T(1024)S(1)} %convert_element_type.143) | copy-start | bytes 9220
  134.7 142.7 %all-reduce.15.cloned.1.call-start = ((), (), s32[]{:S(2)}) async-start(), calls=%async_computation.10 | async-start | bytes 4718592 | tf_op jit(solution)/shard_map/psum | solution.py:113
  201.9 11.5 %copy-start.8 = (f32[2,1536,768]{2,1,0:T(8,128)}, f32[2,1536,768]{2,1,0:T(8,128)S(1)}, u32[]{:S(2)}) copy-start(f32[2,1536,768]{2,1,0:T(8,128)S(1)} %add_bitcast_fusion) | copy-start | bytes 28311556
  201.9 13.0 %copy-start.50 = (bf16[768,768]{1,0:T(8,128)(2,1)S(1)}, bf16[768,768]{1,0:T(8,128)(2,1)}, u32[]{:S(2)}) copy-start(bf16[768,768]{1,0:T(8,128)(2,1)} %param.28) | copy-start | bytes 3538948
  218.4 142.2 %all-reduce.17.cloned.1.call-start = ((), (), s32[]{:S(2)}) async-start(), calls=%async_computation.12 | async-start | bytes 4718592 | tf_op jit(solution)/shard_map/psum | solution.py:131
  281.6 7.5 slice-start
  281.7 7.5 slice-start.3
  289.1 7.2 copy-start.6
  289.1 78.0 %copy-start.25 = (f32[1536]{0:T(1024)}, f32[1536]{0:T(1024)S(1)}, u32[]{:S(2)}) copy-start(f32[1536]{0:T(1024)S(1)} %negate_multiply_fusion.2) | copy-start | bytes 18436
  304.7 196.4 %reduce-scatter.13.cloned.1.call-start = ((), (), s32[]{:S(2)}) async-start(), calls=%async_computation.14 | async-start | bytes 2949120
  360.6 6.5 copy-start.10
  376.9 5.3 copy-start.17
  389.4 11.2 %copy-start.12 = (bf16[3,512,3,64]{1,0,3,2:T(4,128)(2,1)S(1)}, bf16[3,512,3,64]{1,0,3,2:T(4,128)(2,1)}, u32[]{:S(2)}) copy-start(bf16[3,512,3,64]{1,0,3,2:T(4,128)(2,1)} %copy-done.11) | copy-start | bytes 1769476
  407.9 13.8 %copy-start.13 = (bf16[1,1536,192]{1,2,0:T(8,128)(2,1)}, bf16[1,1536,192]{1,2,0:T(8,128)(2,1)S(1)}, u32[]{:S(2)}) copy-start(bf16[1,1536,192]{1,2,0:T(8,128)(2,1)S(1)} %stack.36) | copy-start | bytes 1769476
  412.4 9.3 %copy-start.14 = (bf16[1,1536,192]{1,2,0:T(8,128)(2,1)}, bf16[1,1536,192]{1,2,0:T(8,128)(2,1)S(1)}, u32[]{:S(2)}) copy-start(bf16[1,1536,192]{1,2,0:T(8,128)(2,1)S(1)} %stack.34) | copy-start | bytes 1769476
  421.7 141.7 %reduce-scatter.17.cloned.1.call-start = ((), (), s32[]{:S(2)}) async-start(), calls=%async_computation.16 | async-start | bytes 884736
  426.0 171.4 %reduce-scatter.15.cloned.1.call-start = ((), (), s32[]{:S(2)}) async-start(), calls=%async_computation.15 | async-start | bytes 2211840
  439.7 330.1 %all-reduce.19.cloned.1.call-start = ((), (), s32[]{:S(2)}) async-start(), calls=%async_computation.17 | async-start | bytes 9437184
  457.7 7.6 copy-start.42
  457.7 7.7 copy-start.49
  457.7 7.8 copy-start.30
  457.7 384.7 %reduce-scatter.11.cloned.1.call-start = ((), (), s32[]{:S(2)}) async-start(), calls=%async_computation.13 | async-start | bytes 2654208 | tf_op jit(solution)/shard_map/reduce_scatter | solution.py:178
  467.7 10.7 %copy-start.52 = (u32[32]{0:T(128)S(1)}, u32[32]{0:T(128)}, u32[]{:S(2)}) copy-start(u32[32]{0:T(128)} %constant.120) | copy-start | bytes 388
  467.7 11.9 %copy-start.35 = (f32[768]{0:T(1024)S(1)}, f32[768]{0:T(1024)}, u32[]{:S(2)}) copy-start(f32[768]{0:T(1024)} %get-tuple-element.115) | copy-start | bytes 9220
  473.0 27.0 %all-to-all-start.1 = ((bf16[8,192,192]{2,1,0:T(8,128)(2,1)}), bf16[8,192,192]{2,1,0:T(8,128)(2,1)S(1)}, u32[]{:S(2)}, u32[]{:S(2)}) async-start(bf16[8,192,192]{2,1,0:T(8,128)(2,1)} %bitcast.11), calls=%async_computation.1 | async-start | bytes 1572864 | tf_op jit(solution)/shard_map/all_to_all | solution.py:202
  504.6 10.6 %copy-start.31 = (f32[768]{0:T(1024)S(1)}, f32[768]{0:T(1024)}, u32[]{:S(2)}) copy-start(f32[768]{0:T(1024)} %get-tuple-element.101) | copy-start | bytes 9220
  504.6 10.6 %copy-start.32 = (f32[768]{0:T(1024)S(1)}, f32[768]{0:T(1024)}, u32[]{:S(2)}) copy-start(f32[768]{0:T(1024)} %get-tuple-element.90) | copy-start | bytes 9220
  504.6 10.6 %copy-start.38 = (f32[768]{0:T(1024)S(1)}, f32[768]{0:T(1024)}, u32[]{:S(2)}) copy-start(f32[768]{0:T(1024)} %get-tuple-element.84) | copy-start | bytes 9220
  504.6 10.6 %copy-start.36 = (f32[768]{0:T(1024)S(1)}, f32[768]{0:T(1024)}, u32[]{:S(2)}) copy-start(f32[768]{0:T(1024)} %get-tuple-element.86) | copy-start | bytes 9220
  504.7 10.6 %copy-start.37 = (f32[768]{0:T(1024)S(1)}, f32[768]{0:T(1024)}, u32[]{:S(2)}) copy-start(f32[768]{0:T(1024)} %get-tuple-element.87) | copy-start | bytes 9220
  504.7 337.7 %copy-start.1 = (bf16[2,768,768]{2,1,0:T(8,128)(2,1)S(1)}, bf16[2,768,768]{2,1,0:T(8,128)(2,1)}, u32[]{:S(2)}) copy-start(bf16[2,768,768]{2,1,0:T(8,128)(2,1)} %param.26) | copy-start | bytes 7077892
  510.0 261.7 %all-to-all-start.3 = ((bf16[8,192,192]{2,1,0:T(8,128)(2,1)}), bf16[8,192,192]{2,1,0:T(8,128)(2,1)S(1)}, u32[]{:S(2)}, u32[]{:S(2)}) async-start(bf16[8,192,192]{2,1,0:T(8,128)(2,1)} %bitcast.200), calls=%async_computation.3 | async-start | bytes 1572864 | tf_op jit(solution)/shard_map/all_to_all | solution.py:203
  (23 other events, 81.2 us)
Sparse Core Ops, SparseCore 0:
  38.7 23.0 all-gather.2
  99.0 94.0 all-reduce.12
  195.2 24.1 all-gather.4
  221.7 55.6 all-reduce.14
  304.8 55.7 all-reduce.16
  421.8 32.8 reduce-scatter.12
  458.0 66.9 reduce-scatter.16
  528.5 68.9 reduce-scatter.14
  601.1 168.6 all-reduce.18
  773.7 68.6 reduce-scatter.10
where the time goes:
time: 856 us; the launch traced here: 849 us
  waiting for transfers between devices  487 us (57%)
  local copies, waits for them, and re-layouts  110 us (13%)
  matrix products  82.2 us (10%)
  blocking collectives  71.8 us (8%)
  other arithmetic  66.4 us (8%)
  between operations  16.1 us (2%)
  starting transfers between devices  15.7 us (2%)
    unnamed x14, waiting for transfers between devices  203 us
    reduce_scatter x1, waiting for transfers between devices, on_device(): lax.psum_scatter(g_down * grad_scale, 'dp', scatter_dimension=1, tiled=True)  69.6 us
    psum x1, waiting for transfers between devices, on_device(): attended = lax.psum(attn_part, 'tensor')  58.2 us
    psum x1, waiting for transfers between devices, on_device(): lax.psum(d_normed_part.astype(jnp.bfloat16), 'tensor').astype(jnp.float32)  54.8 us
    psum x1, blocking collectives, on_device(): lax.psum((g_qv_bias * grad_scale, g_up_bias * grad_scale), 'dp')  44.6 us
    psum x1, waiting for transfers between devices, on_device(): lax.psum(ffn_part.astype(jnp.bfloat16), 'tensor').astype(jnp.float32)  43.8 us
    unnamed x135, local copies, waits for them, and re-layouts  31.6 us
    all_to_all x1, blocking collectives, on_device(): lax.all_to_all(tokens, 'dp', split_axis=0, concat_axis=0, tiled=True)  27.3 us
  transfers between devices with their start and end apart: 13, of which 10 were waited for; matrix products, arithmetic and copies ran while one was open for 14% of the time, Pallas kernels for 0%

commit v1 on v0

--- a/solution.py
+++ b/solution.py
@@ -128,7 +128,9 @@
     d_normed_part = jnp.einsum(
         "ktf,kdf->td", d_lifted, up_weight, preferred_element_type=jnp.float32
     )
-    d_normed = d_mixed + lax.psum(d_normed_part.astype(jnp.bfloat16), "tensor").astype(jnp.float32)
+    d_normed = d_mixed + jnp.sum(
+        lax.all_gather(d_normed_part.astype(jnp.bfloat16), "tensor"), axis=0
+    ).astype(jnp.float32)
     d_hidden, d_first_gain, d_first_shift = first_pull(d_normed)
     d_hidden_low = d_hidden.astype(jnp.bfloat16)
     g_out = jnp.einsum("te,td->ed", context, d_hidden_low, preferred_element_type=jnp.float32)

time: 856 us -> 889 us (1.039)
  waiting for transfers between devices: 487 us -> 523 us
  blocking collectives: 71.8 us -> 62.3 us
    all_gather x0 -> x1, waiting for transfers between devices: none -> 64.4 us  [on_device(): lax.all_gather(d_normed_part.astype(jnp.bfloat16), 'tensor')]
    psum x1 -> x0, waiting for transfers between devices: 54.8 us -> none  [on_device(): lax.psum(d_normed_part.astype(jnp.bfloat16), 'tensor').astype(jnp.float32)]
    all_to_all x1, waiting for transfers between devices: 17.3 us -> 37.9 us  [on_device(): lax.all_to_all(layer_back, 'dp', split_axis=0, concat_axis=0, tiled=True)]
    psum x1, blocking collectives: 44.6 us -> 35.1 us  [on_device(): lax.psum((g_qv_bias * grad_scale, g_up_bias * grad_scale), 'dp')]
  transfers between devices with their start and end apart: 13 -> 13, of which waited for: 10 -> 11; matrix products, arithmetic and copies ran while one was open for 14% -> 14% of each run, Pallas kernels for 0% -> 0%
where the time goes in v1:
time: 889 us; the launch traced here: 882 us
  waiting for transfers between devices  523 us (59%)
  local copies, waits for them, and re-layouts  110 us (12%)
  matrix products  84.1 us (9%)
  other arithmetic  71.8 us (8%)
  blocking collectives  62.3 us (7%)
  between operations  16.1 us (2%)
  starting transfers between devices  15.3 us (2%)
    unnamed x14, waiting for transfers between devices  208 us
    reduce_scatter x1, waiting for transfers between devices, on_device(): lax.psum_scatter(g_down * grad_scale, 'dp', scatter_dimension=1, tiled=True)  69.5 us
    all_gather x1, waiting for transfers between devices, on_device(): lax.all_gather(d_normed_part.astype(jnp.bfloat16), 'tensor')  64.4 us
    psum x1, waiting for transfers between devices, on_device(): attended = lax.psum(attn_part, 'tensor')  58.2 us
    psum x1, waiting for transfers between devices, on_device(): lax.psum(ffn_part.astype(jnp.bfloat16), 'tensor').astype(jnp.float32)  43.8 us
    all_to_all x1, waiting for transfers between devices, on_device(): lax.all_to_all(layer_back, 'dp', split_axis=0, concat_axis=0, tiled=True)  37.9 us
    psum x1, blocking collectives, on_device(): lax.psum((g_qv_bias * grad_scale, g_up_bias * grad_scale), 'dp')  35.1 us
    unnamed x135, local copies, waits for them, and re-layouts  31.3 us
  transfers between devices with their start and end apart: 13, of which 11 were waited for; matrix products, arithmetic and copies ran while one was open for 14% of the time, Pallas kernels for 0%

profile of v1, /device:TPU:0, one launch (start us, length us, event | category | flops | bytes accessed | tf_op | source)
XLA Modules:
  0.0 882.3 jit_solution(8722522916748703831)
XLA Ops:
  9.3 27.3 %all_to_all.42 = bf16[8,192,192]{1,2,0:T(8,128)(2,1)S(1)} all-to-all(bf16[8,192,192]{1,2,0:T(8,128)(2,1)S(1)} %copy.124), channel_id=1, replica_groups=mesh['dp'=8,'tensor'=4] {'dp'}, dimensions={0} | all-to-all | bytes 1179648 | tf_op jit(solution)/shard_map/all_to_all | solution.py:63
  42.5 19.2 %all-gather.5.cloned.1.call-done = bf16[1536,768]{0,1:T(8,128)(2,1)} async-done(((bf16[1536,192]{0,1:T(8,128)(2,1)}), bf16[1536,768]{0,1:T(8,128)(2,1)}) %all-gather.5.cloned.1.call-update) | async-done | bytes 2359312 | tf_op jit(solution)/shard_map/all_gather | solution.py:67
  61.7 4.3 copy.126
  66.0 10.1 %scatter_custom_fusion = bf16[1536,768]{1,0:T(8,128)(2,1)} fusion(s32[1536]{0:T(1024)S(1)} %fusion.70, bf16[1536,768]{1,0:T(8,128)(2,1)} %copy.126, bf16[]{:T(256)} %constant.46.clone.1), kind=kCustom, calls=%fused_computation.108 | custom fusion | bytes 2359808 | tf_op jit(solution)/shard_map/scatter | solution.py:71
  76.1 3.2 fusion.86
  84.3 5.3 fusion.85
  95.9 2.9 fusion.87
  103.5 5.5 all-to-all-start.2
  109.2 20.5 %all-to-all-done.2 = bf16[8,192,192]{1,2,0:T(8,128)(2,1)} async-done(((bf16[8,192,192]{1,2,0:T(8,128)(2,1)}), bf16[8,192,192]{1,2,0:T(8,128)(2,1)}, u32[]{:S(2)}, u32[]{:S(2)}) %all-to-all-start.2) | async-done | bytes 589856 | tf_op jit(solution)/shard_map/all_to_all | solution.py:64
  134.9 58.2 %all-reduce.12.cloned.1.call-done = f32[1536,768]{1,0:T(8,128)} async-done(((f32[1536,768]{1,0:T(8,128)}), f32[1536,768]{1,0:T(8,128)}) %all-reduce.12.cloned.1.call-update) | async-done | bytes 4718608 | tf_op jit(solution)/shard_map/psum | solution.py:102
  193.0 3.8 fusion.82
  197.5 4.3 add_bitcast_fusion
  201.8 11.5 %multiply_convert_fusion.2 = (bf16[1536,768]{1,0:T(8,128)(2,1)S(1)}, f32[1536,768]{1,0:T(8,128)}) fusion(f32[2,1536,768]{2,1,0:T(8,128)S(1)} %add_bitcast_fusion), kind=kLoop, calls=%fused_computation.51 | loop fusion | flops 77856768 | bytes 16515072 | tf_op jit(solution)/shard_map/convert_element_type | solution.py:111
  214.8 3.4 convolution_convert_fusion
  219.4 4.3 copy.135
  223.7 9.8 %scatter_custom_fusion.1 = bf16[1536,768]{1,0:T(8,128)(2,1)} fusion(s32[1536]{0:T(1024)S(1)} %fusion.70, bf16[1536,768]{1,0:T(8,128)(2,1)} %copy.135, bf16[]{:T(256)} %constant.46.clone.1), kind=kCustom, calls=%fused_computation.106 | custom fusion | bytes 2359808 | tf_op jit(solution)/shard_map/scatter | solution.py:72
  233.5 43.8 %all-reduce.14.cloned.1.call-done = bf16[1536,768]{1,0:T(8,128)(2,1)} async-done(((bf16[1536,768]{1,0:T(8,128)(2,1)}), bf16[1536,768]{1,0:T(8,128)(2,1)}) %all-reduce.14.cloned.1.call-update) | async-done | bytes 2359312 | tf_op jit(solution)/shard_map/psum | solution.py:113
  277.3 4.3 fusion.80
  284.4 4.6 fusion.79
  289.1 7.1 fusion.36
  297.6 7.0 bitcast_convert_fusion.1
  304.7 64.4 %all-gather.9.cloned.1.call-done = bf16[6144,768]{1,0:T(8,128)(2,1)} async-done(((bf16[1536,768]{1,0:T(8,128)(2,1)}), bf16[6144,768]{1,0:T(8,128)(2,1)}) %all-gather.9.cloned.1.call-update) | async-done | bytes 9437200 | tf_op jit(solution)/shard_map/all_gather | solution.py:132
  369.1 6.7 reduce_sum.183
  375.8 6.3 multiply_reduce_fusion.1
  382.2 4.5 fusion.78
  391.4 6.1 fusion.48
  397.5 7.2 multiply_reduce_fusion
  404.7 11.2 %multiply_convert_fusion = bf16[3,3,512,512]{2,3,1,0:T(8,128)(2,1)} fusion(f32[3,3,512,512]{2,3,1,0:T(8,128)} %get-tuple-element.127, f32[3,3,512,512]{2,3,1,0:T(8,128)} %copy-done.2, f32[3,3,512]{2,1,0:T(4,128)S(1)} %get-tuple-element.126, f32[3,3,512]{2,1,0:T(4,128)S(1)} %log_add_fusion), kind=kLoop, calls=%fused_computation.5 | loop fusion | flops 9437184 | bytes 23629824 | tf_op jit(solution)/shard_map/convert_element_type | solution.py:155
  415.9 4.0 fusion.51
  432.4 4.6 fusion.31
  437.1 10.2 %multiply_bitcast_fusion = f32[2,768,768]{1,2,0:T(8,128)} fusion(bf16[1,1536,768]{2,1,0:T(8,128)(2,1)} %get-tuple-element.114, bf16[1,1536,768]{2,1,0:T(8,128)(2,1)} %copy-done.18, f32[1536,768]{1,0:T(8,128)} %copy-done.3, f32[768]{0:T(1024)S(1)} %copy-done.33, f32[768]{0:T(1024)S(1)} %copy-done.26, f32[1536]{0:T(1024)S(1)} %fusion.68, ...), kind=kOutput, calls=%fused_computation.43 | convolution fusion | flops 3633315840 | bytes 14174208 | tf_op jit(solution)/shard_map/td,ktf->kdf/dot_general | solution.py:126
  447.3 8.3 copy.150
  455.7 3.9 convolution_multiply_fusion.3
  462.0 4.3 multiply_bitcast_fusion.1
  466.2 4.2 copy.162
  470.4 4.8 reshape.284
  475.6 6.0 convolution_multiply_fusion
  483.9 5.4 gather_fusion
  489.3 5.4 all-to-all-start.1
  496.0 3.1 convert_reduce_fusion
  499.2 37.9 %all-to-all-done.1 = bf16[8,192,192]{2,1,0:T(8,128)(2,1)S(1)} async-done(((bf16[8,192,192]{2,1,0:T(8,128)(2,1)}), bf16[8,192,192]{2,1,0:T(8,128)(2,1)S(1)}, u32[]{:S(2)}, u32[]{:S(2)}) %all-to-all-start.1) | async-done | bytes 589856 | tf_op jit(solution)/shard_map/all_to_all | solution.py:204
  541.7 5.4 gather_fusion.1
  547.1 3.6 all-to-all-start.3
  550.7 116.5 %all-reduce.16.cloned.1.call-done = f32[2,768,768]{2,0,1:T(2,128)} async-done(((f32[2,768,768]{2,0,1:T(2,128)}), f32[2,768,768]{2,0,1:T(2,128)}) %all-reduce.16.cloned.1.call-update) | async-done | bytes 4718608
  670.7 35.1 %all-reduce.7 = (f32[2,192]{1,0:T(2,128)}, f32[768]{0:T(1024)S(1)}, f32[768]{0:T(1024)S(1)}, f32[768]{0:T(1024)S(1)}, f32[2,768]{1,0:T(2,128)}, /*index=5*/f32[7...) all-reduce(f32[2,192]{1,0:T(2,128)S(1)} %broadcast_multiply_fusion.10, ...), channel_id=1, replica_groups=mesh['dp'=8,'tensor'=4] {'dp'}, use_global_device_ids=true, to_apply=%region_19.20 | all-reduce | flops 6528 | bytes 52224 | tf_op jit(solution)/shard_map/psum | solution.py:199
  709.3 23.4 %reduce-scatter.17.cloned.1.call-done = f32[96,192]{1,0:T(8,128)} async-done(((f32[768,192]{1,0:T(8,128)}), f32[96,192]{1,0:T(8,128)}) %reduce-scatter.17.cloned.1.call-update) | async-done | bytes 73744
  734.3 68.4 %reduce-scatter.15.cloned.1.call-done = f32[96,576]{1,0:T(8,128)} async-done(((f32[768,576]{1,0:T(8,128)}), f32[96,576]{1,0:T(8,128)}) %reduce-scatter.15.cloned.1.call-update) | async-done | bytes 221200
  805.7 69.5 %reduce-scatter.11.cloned.1.call-done = f32[768,96]{0,1:T(8,128)} async-done(((f32[768,768]{0,1:T(8,128)}), f32[768,96]{0,1:T(8,128)}) %reduce-scatter.11.cloned.1.call-update) | async-done | bytes 294928 | tf_op jit(solution)/shard_map/reduce_scatter | solution.py:180
  (226 shorter events, 75.4 us)
Async XLA Ops:
  7.2 190.4 %copy-start = (bf16[2,768,768]{2,1,0:T(8,128)(2,1)S(1)}, bf16[2,768,768]{2,1,0:T(8,128)(2,1)}, u32[]{:S(2)}) copy-start(bf16[2,768,768]{2,1,0:T(8,128)(2,1)} %param.26) | copy-start | bytes 7077892
  7.2 31.4 %copy-start.37 = (s32[1536]{0:T(1024)S(1)}, s32[1536]{0:T(1024)}, u32[]{:S(2)}) copy-start(s32[1536]{0:T(1024)} %param.18) | copy-start | bytes 18436
  7.2 31.5 %copy-start.38 = (s32[1,1536]{1,0:T(1,128)S(1)}, s32[1,1536]{1,0:T(1,128)}, u32[]{:S(2)}) copy-start(s32[1,1536]{1,0:T(1,128)} %param.19) | copy-start | bytes 18436
  7.2 31.5 %copy-start.41 = (bf16[2,192]{1,0:T(2,128)(2,1)S(1)}, bf16[2,192]{1,0:T(2,128)(2,1)}, u32[]{:S(2)}) copy-start(bf16[2,192]{1,0:T(2,128)(2,1)} %param.21) | copy-start | bytes 2308
  7.2 54.5 %all-gather.5.cloned.1.call-start = ((), (), s32[]{:S(2)}) async-start(), calls=%async_computation.8 | async-start | bytes 2949120 | tf_op jit(solution)/shard_map/all_gather | solution.py:67
  38.5 154.5 %all-reduce.12.cloned.1.call-start = ((), (), s32[]{:S(2)}) async-start(), calls=%async_computation.9 | async-start | bytes 9437184 | tf_op jit(solution)/shard_map/psum | solution.py:102
  38.8 184.9 %copy-start.27 = (s32[1536]{0:T(1024)}, s32[1536]{0:T(1024)S(1)}, u32[]{:S(2)}) copy-start(s32[1536]{0:T(1024)S(1)} %fusion.70) | copy-start | bytes 18436
  42.5 33.6 %copy-start.49 = (bf16[3,768,192]{1,2,0:T(8,128)(2,1)S(1)}, bf16[3,768,192]{1,2,0:T(8,128)(2,1)}, u32[]{:S(2)}) copy-start(bf16[3,768,192]{1,2,0:T(8,128)(2,1)} %param.20) | copy-start | bytes 2654212
  98.8 10.2 %copy-start.43 = (bf16[768]{0:T(1024)(128)(2,1)S(1)}, bf16[768]{0:T(1024)(128)(2,1)}, u32[]{:S(2)}) copy-start(bf16[768]{0:T(1024)(128)(2,1)} %param.24) | copy-start | bytes 4612
  98.8 10.3 %copy-start.44 = (bf16[768]{0:T(1024)(128)(2,1)S(1)}, bf16[768]{0:T(1024)(128)(2,1)}, u32[]{:S(2)}) copy-start(bf16[768]{0:T(1024)(128)(2,1)} %param.25) | copy-start | bytes 4612
  98.8 10.3 %copy-start.45 = (bf16[768]{0:T(1024)(128)(2,1)S(1)}, bf16[768]{0:T(1024)(128)(2,1)}, u32[]{:S(2)}) copy-start(bf16[768]{0:T(1024)(128)(2,1)} %param.23) | copy-start | bytes 4612
  98.8 10.3 %copy-start.42 = (bf16[2,768]{1,0:T(2,128)(2,1)S(1)}, bf16[2,768]{1,0:T(2,128)(2,1)}, u32[]{:S(2)}) copy-start(bf16[2,768]{1,0:T(2,128)(2,1)} %param.27) | copy-start | bytes 9220
  103.5 26.2 %all-to-all-start.2 = ((bf16[8,192,192]{1,2,0:T(8,128)(2,1)}), bf16[8,192,192]{1,2,0:T(8,128)(2,1)}, u32[]{:S(2)}, u32[]{:S(2)}) async-start(bf16[8,192,192]{1,2,0:T(8,128)(2,1)} %copy.133), calls=%async_computation.2 | async-start | bytes 1572864 | tf_op jit(solution)/shard_map/all_to_all | solution.py:64
  109.0 110.4 %all-gather.7.cloned.1.call-start = ((), (), s32[]{:S(2)}) async-start(), calls=%async_computation.11 | async-start | bytes 2949120 | tf_op jit(solution)/shard_map/all_gather | solution.py:68
  109.1 168.2 %copy-start.24 = (f32[768]{0:T(1024)}, f32[768]{0:T(1024)S(1)}, u32[]{:S(2)}) copy-start(f32[768]{0:T(1024)S(1)} %convert_element_type.144) | copy-start | bytes 9220
  109.1 168.2 %copy-start.32 = (f32[768]{0:T(1024)}, f32[768]{0:T(1024)S(1)}, u32[]{:S(2)}) copy-start(f32[768]{0:T(1024)S(1)} %convert_element_type.145) | copy-start | bytes 9220
  134.6 142.7 %all-reduce.14.cloned.1.call-start = ((), (), s32[]{:S(2)}) async-start(), calls=%async_computation.10 | async-start | bytes 4718592 | tf_op jit(solution)/shard_map/psum | solution.py:113
  201.8 11.5 %copy-start.8 = (f32[2,1536,768]{2,1,0:T(8,128)}, f32[2,1536,768]{2,1,0:T(8,128)S(1)}, u32[]{:S(2)}) copy-start(f32[2,1536,768]{2,1,0:T(8,128)S(1)} %add_bitcast_fusion) | copy-start | bytes 28311556
  201.8 13.0 %copy-start.48 = (bf16[768,768]{1,0:T(8,128)(2,1)S(1)}, bf16[768,768]{1,0:T(8,128)(2,1)}, u32[]{:S(2)}) copy-start(bf16[768,768]{1,0:T(8,128)(2,1)} %param.28) | copy-start | bytes 3538948
  218.3 150.8 %all-gather.9.cloned.1.call-start = ((), (), s32[]{:S(2)}) async-start(), calls=%async_computation.13 | async-start | bytes 11796480 | tf_op jit(solution)/shard_map/all_gather | solution.py:132
  281.6 7.4 slice-start.2
  281.6 7.4 slice-start.5
  289.0 7.2 copy-start.6
  304.6 233.5 %reduce-scatter.13.cloned.1.call-start = ((), (), s32[]{:S(2)}) async-start(), calls=%async_computation.14 | async-start | bytes 2949120
  369.1 6.7 copy-start.25
  369.1 13.1 %slice-start = ((s8[4718592]{0:T(1024)(128)(4,1)}), s8[524288]{0:T(1024)(128)(4,1)S(1)}, s32[]{:S(2)}) async-start(s8[4718592]{0:T(1024)(128)(4,1)} %bitcast.189), calls=%async_computation.18 | async-start | bytes 1048576
  375.8 6.4 slice-start.1
  404.7 11.2 %copy-start.11 = (bf16[3,512,3,64]{1,0,3,2:T(4,128)(2,1)S(1)}, bf16[3,512,3,64]{1,0,3,2:T(4,128)(2,1)}, u32[]{:S(2)}) copy-start(bf16[3,512,3,64]{1,0,3,2:T(4,128)(2,1)} %copy-done.10) | copy-start | bytes 1769476
  423.0 13.9 %copy-start.12 = (bf16[1,1536,192]{1,2,0:T(8,128)(2,1)}, bf16[1,1536,192]{1,2,0:T(8,128)(2,1)S(1)}, u32[]{:S(2)}) copy-start(bf16[1,1536,192]{1,2,0:T(8,128)(2,1)S(1)} %stack.36) | copy-start | bytes 1769476
  427.7 9.3 %copy-start.13 = (bf16[1,1536,192]{1,2,0:T(8,128)(2,1)}, bf16[1,1536,192]{1,2,0:T(8,128)(2,1)S(1)}, u32[]{:S(2)}) copy-start(bf16[1,1536,192]{1,2,0:T(8,128)(2,1)S(1)} %stack.34) | copy-start | bytes 1769476
  437.0 230.1 %all-reduce.16.cloned.1.call-start = ((), (), s32[]{:S(2)}) async-start(), calls=%async_computation.17 | async-start | bytes 9437184
  455.6 6.3 copy-start.9
  455.6 277.1 %reduce-scatter.17.cloned.1.call-start = ((), (), s32[]{:S(2)}) async-start(), calls=%async_computation.16 | async-start | bytes 884736
  461.9 340.8 %reduce-scatter.15.cloned.1.call-start = ((), (), s32[]{:S(2)}) async-start(), calls=%async_computation.15 | async-start | bytes 2211840
  475.3 6.3 copy-start.40
  475.3 6.4 copy-start.47
  475.3 6.4 copy-start.28
  475.3 399.9 %reduce-scatter.11.cloned.1.call-start = ((), (), s32[]{:S(2)}) async-start(), calls=%async_computation.12 | async-start | bytes 2654208 | tf_op jit(solution)/shard_map/reduce_scatter | solution.py:180
  483.9 10.8 %copy-start.50 = (u32[32]{0:T(128)S(1)}, u32[32]{0:T(128)}, u32[]{:S(2)}) copy-start(u32[32]{0:T(128)} %constant.121) | copy-start | bytes 388
  483.9 12.1 %copy-start.31 = (f32[768]{0:T(1024)S(1)}, f32[768]{0:T(1024)}, u32[]{:S(2)}) copy-start(f32[768]{0:T(1024)} %get-tuple-element.115) | copy-start | bytes 9220
  489.3 47.8 %all-to-all-start.1 = ((bf16[8,192,192]{2,1,0:T(8,128)(2,1)}), bf16[8,192,192]{2,1,0:T(8,128)(2,1)S(1)}, u32[]{:S(2)}, u32[]{:S(2)}) async-start(bf16[8,192,192]{2,1,0:T(8,128)(2,1)} %bitcast.11), calls=%async_computation.1 | async-start | bytes 1572864 | tf_op jit(solution)/shard_map/all_to_all | solution.py:204
  541.7 128.9 %copy-start.29 = (f32[768]{0:T(1024)S(1)}, f32[768]{0:T(1024)}, u32[]{:S(2)}) copy-start(f32[768]{0:T(1024)} %get-tuple-element.101) | copy-start | bytes 9220
  541.7 129.0 %copy-start.30 = (f32[768]{0:T(1024)S(1)}, f32[768]{0:T(1024)}, u32[]{:S(2)}) copy-start(f32[768]{0:T(1024)} %get-tuple-element.90) | copy-start | bytes 9220
  541.7 129.0 %copy-start.36 = (f32[768]{0:T(1024)S(1)}, f32[768]{0:T(1024)}, u32[]{:S(2)}) copy-start(f32[768]{0:T(1024)} %get-tuple-element.84) | copy-start | bytes 9220
  541.7 129.0 %copy-start.34 = (f32[768]{0:T(1024)S(1)}, f32[768]{0:T(1024)}, u32[]{:S(2)}) copy-start(f32[768]{0:T(1024)} %get-tuple-element.86) | copy-start | bytes 9220
  541.7 129.0 %copy-start.35 = (f32[768]{0:T(1024)S(1)}, f32[768]{0:T(1024)}, u32[]{:S(2)}) copy-start(f32[768]{0:T(1024)} %get-tuple-element.87) | copy-start | bytes 9220
  541.7 333.5 %copy-start.1 = (bf16[2,768,768]{2,1,0:T(8,128)(2,1)S(1)}, bf16[2,768,768]{2,1,0:T(8,128)(2,1)}, u32[]{:S(2)}) copy-start(bf16[2,768,768]{2,1,0:T(8,128)(2,1)} %param.26) | copy-start | bytes 7077892
  547.1 257.5 %all-to-all-start.3 = ((bf16[8,192,192]{2,1,0:T(8,128)(2,1)}), bf16[8,192,192]{2,1,0:T(8,128)(2,1)S(1)}, u32[]{:S(2)}, u32[]{:S(2)}) async-start(bf16[8,192,192]{2,1,0:T(8,128)(2,1)} %bitcast.204), calls=%async_computation.3 | async-start | bytes 1572864 | tf_op jit(solution)/shard_map/all_to_all | solution.py:205
  (23 other events, 85.6 us)
Sparse Core Ops, SparseCore 0:
  38.7 23.0 all-gather.4
  99.0 94.0 all-reduce.11
  195.2 24.1 all-gather.6
  221.6 55.6 all-reduce.13
  304.7 64.2 all-gather.8
  437.1 32.8 reduce-scatter.12
  473.6 193.5 all-reduce.15
  670.4 62.2 reduce-scatter.16
  736.2 66.4 reduce-scatter.14
  806.6 68.5 reduce-scatter.10
